TPU v7x, 32 devices: a whole 2x2x4 slice. The times are simulated.
32 devices in a mesh: row: 2 (over core), col: 4 (over z), depth: 4 (over y, x).
Axes of the slice: x: 2, y: 2, z: 4, core: 2. Of those that a mesh axis runs over, the one named last changes fastest.
Arguments:
- tokens: bfloat16 [768, 4096], P(('col', 'depth'), 'row'), may hold values from -6 to 6
- cotangent: bfloat16 [768, 4096], P(('col', 'depth'), 'row'), may hold values from -6 to 6
- gate_weight: bfloat16 [4096, 14336], P(('row', 'depth'), 'col'), may hold values from -0.09375 to 0.09375
- up_weight: bfloat16 [4096, 14336], P(('row', 'depth'), 'col'), may hold values from -0.09375 to 0.09375
- down_weight: bfloat16 [14336, 4096], P('col', ('row', 'depth')), may hold values from -0.046875 to 0.046875
Outputs:
- output: bfloat16 [768, 4096], P(('col', 'depth'), 'row')
- input_grad: bfloat16 [768, 4096], P(('col', 'depth'), 'row')
- gate_grad: float32 [4096, 14336], P(('row', 'depth'), 'col')
- up_grad: float32 [4096, 14336], P(('row', 'depth'), 'col')
- down_grad: float32 [14336, 4096], P('col', ('row', 'depth'))
All inputs are finite; a program needn't handle non-finite values.
Results may differ from a plain program's by a relative error of at most 0.0049.
Values may be sent and summed in bfloat16 or wider, within the bound.
No kernel may reach another device: no remote copies, remote signals or barrier semaphores. Data moves between devices by JAX's collectives and lax.ppermute only.
A program may use at most 192 MiB of HBM per device.

v0:
```python
import jax
import jax.numpy as jnp
from jax import lax
from jax.sharding import PartitionSpec as P


def dot_tn(left, right):
    return lax.dot_general(
        left, right, (((0,), (0,)), ((), ())), preferred_element_type=jnp.float32
    )


def dot_nt(left, right):
    return lax.dot_general(
        left, right, (((1,), (1,)), ((), ())), preferred_element_type=jnp.float32
    )


def deltas(hidden_grad, gate, up):
    sig = jax.nn.sigmoid(gate)
    gate_delta = (hidden_grad * up * sig * (1.0 + gate * (1.0 - sig))).astype(jnp.bfloat16)
    up_delta = (hidden_grad * gate * sig).astype(jnp.bfloat16)
    return (gate_delta, up_delta)


def activate(gate, up):
    return (gate * jax.nn.sigmoid(gate) * up).astype(jnp.bfloat16)


def on_device(tokens, cotangent, gate_weight, up_weight, down_weight):
    gate_full, up_full = (
        lax.all_gather(gate_weight, "depth", axis=0, tiled=True),
        lax.all_gather(up_weight, "depth", axis=0, tiled=True),
    )
    down_full = lax.all_gather(down_weight, "depth", axis=1, tiled=True)
    tok_rows, cot_rows = (
        lax.all_gather(tokens, "col", axis=0, tiled=True),
        lax.all_gather(cotangent, "col", axis=0, tiled=True),
    )
    gate = lax.psum_scatter(
        jnp.dot(tok_rows, gate_full, preferred_element_type=jnp.float32),
        "row",
        scatter_dimension=0,
        tiled=True,
    )
    up = lax.psum_scatter(
        jnp.dot(tok_rows, up_full, preferred_element_type=jnp.float32),
        "row",
        scatter_dimension=0,
        tiled=True,
    )
    hid_rows = lax.all_gather(activate(gate, up), "row", axis=0, tiled=True)
    hidden_grad = lax.psum_scatter(
        dot_nt(cot_rows, down_full), "row", scatter_dimension=0, tiled=True
    )
    gate_delta, up_delta = deltas(hidden_grad, gate, up)
    gd_rows, ud_rows = (
        lax.all_gather(gate_delta, "row", axis=0, tiled=True),
        lax.all_gather(up_delta, "row", axis=0, tiled=True),
    )
    output = lax.psum_scatter(
        jnp.dot(hid_rows, down_full, preferred_element_type=jnp.float32),
        "col",
        scatter_dimension=0,
        tiled=True,
    ).astype(jnp.bfloat16)
    input_grad = lax.psum_scatter(
        dot_nt(gd_rows, gate_full) + dot_nt(ud_rows, up_full),
        "col",
        scatter_dimension=0,
        tiled=True,
    ).astype(jnp.bfloat16)
    tok_part, cot_part = (
        lax.all_to_all(tok_rows, "depth", split_axis=1, concat_axis=0, tiled=True),
        lax.all_to_all(cot_rows, "depth", split_axis=1, concat_axis=0, tiled=True),
    )
    gd_all, ud_all, hid_all = (
        lax.all_gather(gd_rows, "depth", axis=0, tiled=True),
        lax.all_gather(ud_rows, "depth", axis=0, tiled=True),
        lax.all_gather(hid_rows, "depth", axis=0, tiled=True),
    )
    gate_grad = dot_tn(tok_part, gd_all)
    up_grad = dot_tn(tok_part, ud_all)
    down_grad = dot_tn(hid_all, cot_part)
    return (output, input_grad, gate_grad, up_grad, down_grad)


def solution(mesh):
    return jax.shard_map(
        on_device,
        mesh=mesh,
        in_specs=(
            P(("col", "depth"), "row"),
            P(("col", "depth"), "row"),
            P(("row", "depth"), "col"),
            P(("row", "depth"), "col"),
            P("col", ("row", "depth")),
        ),
        out_specs=(
            P(("col", "depth"), "row"),
            P(("col", "depth"), "row"),
            P(("row", "depth"), "col"),
            P(("row", "depth"), "col"),
            P("col", ("row", "depth")),
        ),
        check_vma=False,
    )
```

profile of v0, /device:TPU:0, one launch (start us, length us, event | category | flops | bytes accessed | tf_op | source)
XLA Modules:
  0.0 807.5 jit_solution(1116714497966719239)
XLA Ops:
  7.2 0.0 all-gather.10.cloned.1.call-start
  7.2 0.7 all-gather.10.cloned.1.call-update
  7.9 0.0 all-gather.12.cloned.1.call-start
  7.9 0.7 all-gather.12.cloned.1.call-update
  8.7 0.0 all-gather.16.cloned.1.call-start
  8.7 0.7 all-gather.16.cloned.1.call-update
  9.4 0.0 reduce-scatter.6.cloned.1.call-start
  9.4 0.1 copy-done
  9.6 21.3 %all_gather.33 = bf16[192,2048]{1,0:T(8,128)(2,1)S(1)} all-gather(bf16[48,2048]{1,0:T(8,128)(2,1)S(1)} %copy-done), channel_id=1, replica_groups=mesh['row'=2,'col'=4,'depth'=4] {'col'}, dimensions={0}, use_global_device_ids=true | all-gather | bytes 983040 | tf_op jit(solution)/shard_map/all_gather | solution.py:37
  30.9 121.7 %all-gather.10.cloned.1.call-done = bf16[2048,3584]{1,0:T(8,128)(2,1)} async-done(((bf16[512,3584]{1,0:T(8,128)(2,1)}), bf16[2048,3584]{1,0:T(8,128)(2,1)}) %all-gather.10.cloned.1.call-update) | async-done | bytes 14680080 | tf_op jit(solution)/shard_map/all_gather | solution.py:32
  152.5 9.8 %fusion = f32[192,3584]{1,0:T(8,128)} fusion(bf16[192,2048]{1,0:T(8,128)(2,1)S(1)} %all_gather.33, bf16[2048,3584]{1,0:T(8,128)(2,1)} %all-gather.10.cloned.1.call-done), kind=kOutput, calls=%fused_computation.9 | convolution fusion | flops 2818572288 | bytes 18219008 | tf_op jit(solution)/shard_map/dot_general | solution.py:41
  162.3 0.0 reduce-scatter.6.cloned.1.call-update
  162.4 0.0 reduce-scatter.8.cloned.1.call-start
  162.4 132.0 %all-gather.12.cloned.1.call-done = bf16[2048,3584]{1,0:T(8,128)(2,1)} async-done(((bf16[512,3584]{1,0:T(8,128)(2,1)}), bf16[2048,3584]{1,0:T(8,128)(2,1)}) %all-gather.12.cloned.1.call-update) | async-done | bytes 14680080 | tf_op jit(solution)/shard_map/all_gather | solution.py:33
  294.4 9.8 %fusion.1 = f32[192,3584]{1,0:T(8,128)} fusion(bf16[192,2048]{1,0:T(8,128)(2,1)S(1)} %all_gather.33, bf16[2048,3584]{1,0:T(8,128)(2,1)} %all-gather.12.cloned.1.call-done), kind=kOutput, calls=%fused_computation.10 | convolution fusion | flops 2818572288 | bytes 18219008 | tf_op jit(solution)/shard_map/dot_general | solution.py:47
  304.2 0.0 reduce-scatter.8.cloned.1.call-update
  304.2 0.0 reduce-scatter.12.cloned.1.call-start
  304.3 0.9 copy-done.1
  305.2 19.5 %all_gather.38 = bf16[192,2048]{1,0:T(8,128)(2,1)S(1)} all-gather(bf16[48,2048]{1,0:T(8,128)(2,1)S(1)} %copy-done.1), channel_id=1, replica_groups=mesh['row'=2,'col'=4,'depth'=4] {'col'}, dimensions={0}, use_global_device_ids=true | all-gather | bytes 983040 | tf_op jit(solution)/shard_map/all_gather | solution.py:38
  324.7 111.3 %all-gather.16.cloned.1.call-done = bf16[3584,2048]{1,0:T(8,128)(2,1)} async-done(((bf16[3584,512]{1,0:T(8,128)(2,1)}), bf16[3584,2048]{1,0:T(8,128)(2,1)}) %all-gather.16.cloned.1.call-update) | async-done | bytes 14680080 | tf_op jit(solution)/shard_map/all_gather | solution.py:35
  436.1 11.7 %fusion.3 = f32[192,3584]{1,0:T(8,128)} fusion(bf16[192,2048]{1,0:T(8,128)(2,1)S(1)} %all_gather.38, bf16[3584,2048]{1,0:T(8,128)(2,1)} %all-gather.16.cloned.1.call-done), kind=kOutput, calls=%fused_computation.12 | convolution fusion | flops 2818572288 | bytes 18219008 | tf_op jit(solution)/shard_map/dot_general | solution.py:14
  447.8 0.0 reduce-scatter.12.cloned.1.call-update
  447.8 0.0 all-gather.18.cloned.1.call-start
  447.8 1.3 reduce-scatter.6.cloned.1.call-done
  449.1 14.3 %reduce-scatter.8.cloned.1.call-done = f32[96,3584]{1,0:T(8,128)} async-done(((f32[192,3584]{1,0:T(8,128)}), f32[96,3584]{1,0:T(8,128)}) %reduce-scatter.8.cloned.1.call-update) | async-done | bytes 1376272 | tf_op jit(solution)/shard_map/reduce_scatter | solution.py:46
  463.5 14.3 %reduce-scatter.12.cloned.1.call-done = f32[96,3584]{1,0:T(8,128)} async-done(((f32[192,3584]{1,0:T(8,128)}), f32[96,3584]{1,0:T(8,128)}) %reduce-scatter.12.cloned.1.call-update) | async-done | bytes 1376272 | tf_op jit(solution)/shard_map/reduce_scatter | solution.py:53
  477.8 4.2 multiply_convert_fusion
  482.0 0.0 all-gather.18.cloned.1.call-update
  482.0 0.0 all-gather.20.cloned.1.call-start
  482.1 0.7 all-gather.20.cloned.1.call-update
  482.8 0.0 all-gather.14.cloned.1.call-start
  482.8 0.7 all-gather.14.cloned.1.call-update
  483.5 0.2 reduce-scatter.14.cloned.1.call-start
  483.7 9.2 %all-gather.18.cloned.1.call-done = bf16[192,3584]{1,0:T(8,128)(2,1)} async-done(((bf16[96,3584]{1,0:T(8,128)(2,1)}), bf16[192,3584]{1,0:T(8,128)(2,1)}) %all-gather.18.cloned.1.call-update) | async-done | bytes 1376272 | tf_op jit(solution)/shard_map/all_gather | solution.py:58
  492.9 8.5 %fusion.4 = f32[192,2048]{1,0:T(8,128)S(1)} fusion(bf16[192,3584]{1,0:T(8,128)(2,1)} %all-gather.18.cloned.1.call-done, bf16[2048,3584]{1,0:T(8,128)(2,1)} %all-gather.10.cloned.1.call-done), kind=kOutput, calls=%fused_computation.13 | convolution fusion | flops 2818572288 | bytes 17629184 | tf_op jit(solution)/shard_map/dot_general | solution.py:14
  501.4 4.5 all-gather.20.cloned.1.call-done
  505.9 11.6 %convolution_add_fusion = f32[192,2048]{1,0:T(8,128)} fusion(f32[192,2048]{1,0:T(8,128)S(1)} %fusion.4, bf16[192,3584]{1,0:T(8,128)(2,1)} %all-gather.20.cloned.1.call-done, bf16[2048,3584]{1,0:T(8,128)(2,1)} %all-gather.12.cloned.1.call-done), kind=kOutput, calls=%fused_computation.2 | convolution fusion | flops 2818965504 | bytes 19202048 | tf_op jit(solution)/shard_map/dot_general | solution.py:14
  517.5 0.0 reduce-scatter.14.cloned.1.call-update
  517.6 0.0 reduce-scatter.10.cloned.1.call-start
  517.6 1.2 all-gather.14.cloned.1.call-done
  518.8 9.8 %fusion.2 = f32[192,2048]{1,0:T(8,128)} fusion(bf16[192,3584]{1,0:T(8,128)(2,1)} %all-gather.14.cloned.1.call-done, bf16[3584,2048]{1,0:T(8,128)(2,1)} %all-gather.16.cloned.1.call-done), kind=kOutput, calls=%fused_computation.11 | convolution fusion | flops 2818572288 | bytes 17629184 | tf_op jit(solution)/shard_map/dot_general | solution.py:62
  528.6 0.0 reduce-scatter.10.cloned.1.call-update
  528.6 0.0 all-gather.22.cloned.1.call-start
  528.7 0.5 all-gather.22.cloned.1.call-update
  529.2 0.0 all-gather.24.cloned.1.call-start
  529.2 0.7 all-gather.24.cloned.1.call-update
  529.9 0.0 all-gather.26.cloned.1.call-start
  530.0 0.5 all-gather.26.cloned.1.call-update
  530.5 1.0 copy.27
  531.5 3.9 all-to-all-start
  535.4 1.0 copy.26
  536.3 21.8 %reduce-scatter.14.cloned.1.call-done = f32[48,2048]{1,0:T(8,128)} async-done(((f32[192,2048]{1,0:T(8,128)}), f32[48,2048]{1,0:T(8,128)}) %reduce-scatter.14.cloned.1.call-update) | async-done | bytes 393232 | tf_op jit(solution)/shard_map/reduce_scatter | solution.py:67
  558.1 1.7 convert_element_type.19
  559.8 35.6 %reduce-scatter.10.cloned.1.call-done = f32[48,2048]{1,0:T(8,128)} async-done(((f32[192,2048]{1,0:T(8,128)}), f32[48,2048]{1,0:T(8,128)}) %reduce-scatter.10.cloned.1.call-update) | async-done | bytes 393232 | tf_op jit(solution)/shard_map/reduce_scatter | solution.py:61
  595.4 1.7 convert_element_type.16
  597.1 3.7 all-to-all-start.1
  600.8 61.3 %all-gather.22.cloned.1.call-done = bf16[768,3584]{1,0:T(8,128)(2,1)} async-done(((bf16[192,3584]{1,0:T(8,128)(2,1)}), bf16[768,3584]{1,0:T(8,128)(2,1)}) %all-gather.22.cloned.1.call-update) | async-done | bytes 5505040 | tf_op jit(solution)/shard_map/all_gather | solution.py:78
  662.1 7.7 convolution_bitcast_fusion.1
  669.8 8.8 %copy.20 = f32[512,3584]{1,0:T(8,128)} copy(f32[512,3584]{0,1:T(8,128)} %convolution_bitcast_fusion.1) | data formatting | bytes 14680064
  678.6 49.2 %all-gather.24.cloned.1.call-done = bf16[768,3584]{1,0:T(8,128)(2,1)} async-done(((bf16[192,3584]{1,0:T(8,128)(2,1)}), bf16[768,3584]{1,0:T(8,128)(2,1)}) %all-gather.24.cloned.1.call-update) | async-done | bytes 5505040 | tf_op jit(solution)/shard_map/all_gather | solution.py:79
  727.8 7.7 convolution_bitcast_fusion
  735.4 8.7 %copy.21 = f32[512,3584]{1,0:T(8,128)} copy(f32[512,3584]{0,1:T(8,128)} %convolution_bitcast_fusion) | data formatting | bytes 14680064
  744.2 49.1 %all-gather.26.cloned.1.call-done = bf16[768,3584]{1,0:T(8,128)(2,1)} async-done(((bf16[192,3584]{1,0:T(8,128)(2,1)}), bf16[768,3584]{1,0:T(8,128)(2,1)}) %all-gather.26.cloned.1.call-update) | async-done | bytes 5505040 | tf_op jit(solution)/shard_map/all_gather | solution.py:80
  793.2 7.7 fusion.5
  (4 shorter events, 0.0 us)
Async XLA Ops:
  7.2 145.4 %all-gather.10.cloned.1.call-start = ((), (), s32[]{:S(2)}) async-start(), calls=%async_computation.7 | async-start | bytes 18350080 | tf_op jit(solution)/shard_map/all_gather | solution.py:32
  7.9 286.5 %all-gather.12.cloned.1.call-start = ((), (), s32[]{:S(2)}) async-start(), calls=%async_computation.9 | async-start | bytes 18350080 | tf_op jit(solution)/shard_map/all_gather | solution.py:33
  8.6 0.9 copy-start
  8.7 427.4 %all-gather.16.cloned.1.call-start = ((), (), s32[]{:S(2)}) async-start(), calls=%async_computation.12 | async-start | bytes 18350080 | tf_op jit(solution)/shard_map/all_gather | solution.py:35
  9.4 439.7 %reduce-scatter.6.cloned.1.call-start = ((), (), s32[]{:S(2)}) async-start(), calls=%async_computation.8 | async-start | bytes 4128768 | tf_op jit(solution)/shard_map/reduce_scatter | solution.py:40
  162.4 301.1 %reduce-scatter.8.cloned.1.call-start = ((), (), s32[]{:S(2)}) async-start(), calls=%async_computation.10 | async-start | bytes 4128768 | tf_op jit(solution)/shard_map/reduce_scatter | solution.py:46
  304.2 1.0 copy-start.1
  304.2 173.5 %reduce-scatter.12.cloned.1.call-start = ((), (), s32[]{:S(2)}) async-start(), calls=%async_computation.14 | async-start | bytes 4128768 | tf_op jit(solution)/shard_map/reduce_scatter | solution.py:53
  447.8 45.2 %all-gather.18.cloned.1.call-start = ((), (), s32[]{:S(2)}) async-start(), calls=%async_computation.15 | async-start | bytes 2064384 | tf_op jit(solution)/shard_map/all_gather | solution.py:58
  482.0 23.9 %all-gather.20.cloned.1.call-start = ((), (), s32[]{:S(2)}) async-start(), calls=%async_computation.16 | async-start | bytes 2064384 | tf_op jit(solution)/shard_map/all_gather | solution.py:59
  482.8 36.1 %all-gather.14.cloned.1.call-start = ((), (), s32[]{:S(2)}) async-start(), calls=%async_computation.11 | async-start | bytes 2064384 | tf_op jit(solution)/shard_map/all_gather | solution.py:52
  483.5 74.6 %reduce-scatter.14.cloned.1.call-start = ((), (), s32[]{:S(2)}) async-start(), calls=%async_computation.17 | async-start | bytes 1966080 | tf_op jit(solution)/shard_map/reduce_scatter | solution.py:67
  517.6 77.9 %reduce-scatter.10.cloned.1.call-start = ((), (), s32[]{:S(2)}) async-start(), calls=%async_computation.13 | async-start | bytes 1966080 | tf_op jit(solution)/shard_map/reduce_scatter | solution.py:61
  528.6 133.5 %all-gather.22.cloned.1.call-start = ((), (), s32[]{:S(2)}) async-start(), calls=%async_computation.18 | async-start | bytes 6881280 | tf_op jit(solution)/shard_map/all_gather | solution.py:78
  529.2 198.6 %all-gather.24.cloned.1.call-start = ((), (), s32[]{:S(2)}) async-start(), calls=%async_computation.19 | async-start | bytes 6881280 | tf_op jit(solution)/shard_map/all_gather | solution.py:79
  529.9 263.3 %all-gather.26.cloned.1.call-start = ((), (), s32[]{:S(2)}) async-start(), calls=%async_computation.20 | async-start | bytes 6881280 | tf_op jit(solution)/shard_map/all_gather | solution.py:80
  531.5 65.6 %all-to-all-start = ((bf16[192,4,512]{2,0,1:T(8,128)(2,1)}), bf16[192,4,512]{2,0,1:T(8,128)(2,1)S(1)}, u32[]{:S(2)}, u32[]{:S(2)}) async-start(bf16[192,4,512]{2,0,1:T(8,128)(2,1)} %bitcast.35), calls=%async_computation.5 | async-start | bytes 1572864 | tf_op jit(solution)/shard_map/all_to_all | solution.py:74
  597.1 147.1 %all-to-all-start.1 = ((bf16[192,4,512]{2,0,1:T(8,128)(2,1)}), bf16[192,4,512]{2,0,1:T(8,128)(2,1)S(1)}, u32[]{:S(2)}, u32[]{:S(2)}) async-start(bf16[192,4,512]{2,0,1:T(8,128)(2,1)} %bitcast.34), calls=%async_computation.6 | async-start | bytes 1572864 | tf_op jit(solution)/shard_map/all_to_all | solution.py:75
Sparse Core Ops, SparseCore 0:
  9.8 142.6 all-gather.9
  154.4 139.9 all-gather.11
  296.2 139.8 all-gather.15
  438.8 10.3 reduce-scatter.5
  451.9 11.5 reduce-scatter.7
  466.1 11.5 reduce-scatter.11
  482.1 10.7 all-gather.17
  495.1 10.7 all-gather.19
  508.1 10.6 all-gather.13
  521.7 36.4 reduce-scatter.13
  561.1 34.2 reduce-scatter.9
  597.3 64.8 all-gather.21
  664.1 63.6 all-gather.23
  729.6 63.6 all-gather.25
where the time goes:
time: 808 us; the launch traced here: 807 us
  waiting for transfers between devices  632 us (78%)
  matrix products  84.2 us (10%)
  blocking collectives  40.8 us (5%)
  local copies, waits for them, and re-layouts  20.5 us (3%)
  between operations  14 us (2%)
  starting transfers between devices  8.36 us (1%)
    all_gather x1, waiting for transfers between devices, on_device(): lax.all_gather(up_weight, 'depth', axis=0, tiled=True)  132 us
    all_gather x1, waiting for transfers between devices, on_device(): lax.all_gather(gate_weight, 'depth', axis=0, tiled=True)  122 us
    all_gather x1, waiting for transfers between devices, on_device(): down_full = lax.all_gather(down_weight, 'depth', axis=1, tiled=True)  111 us
    all_gather x1, waiting for transfers between devices, on_device(): lax.all_gather(gd_rows, 'depth', axis=0, tiled=True)  61.3 us
    all_gather x1, waiting for transfers between devices, on_device(): lax.all_gather(ud_rows, 'depth', axis=0, tiled=True)  49.2 us
    all_gather x1, waiting for transfers between devices, on_device(): lax.all_gather(hid_rows, 'depth', axis=0, tiled=True)  49.1 us
    reduce_scatter x1, waiting for transfers between devices, on_device(): lax.psum_scatter(jnp.dot(hid_rows, down_full, preferred_element_type=jnp....  35.6 us
    dot_general x3, matrix products, dot_nt(): lax.dot_general(left, right, (((1,), (1,)), ((), ())), preferred_element_...  31.8 us
  transfers between devices with their start and end apart: 16, of which 14 were waited for; matrix products, arithmetic and copies ran while one was open for 12% of the time, Pallas kernels for 0%

commit v1 on v0

--- a/solution.py
+++ b/solution.py
@@ -2,6 +2,28 @@
 import jax.numpy as jnp
 from jax import lax
 from jax.sharding import PartitionSpec as P
+
+
+def joined_along(blocks, dim):
+    lengths = list(blocks.shape[1:])
+    lengths[dim] *= blocks.shape[0]
+    return jnp.moveaxis(blocks, 0, dim).reshape(lengths)
+
+
+def ring_gather(x, axis, dim):
+    count = lax.axis_size(axis)
+    pairs = [(i, (i + 1) % count) for i in range(count)]
+    back = [(b, a) for a, b in pairs]
+    lower, upper = ([], [])
+    for turn in range(count - 1):
+        if turn % 2 == 0:
+            lower.append(lax.ppermute(lower[-1] if lower else x, axis, pairs))
+        else:
+            upper.append(lax.ppermute(upper[-1] if upper else x, axis, back))
+    blocks = jnp.stack([*lower[::-1], x, *upper])
+    shift = lax.axis_index(axis) - len(lower)
+    blocks = blocks[(jnp.arange(count) - shift) % count]
+    return joined_along(blocks, dim)
 
 
 def dot_tn(left, right):
@@ -75,7 +97,7 @@
         lax.all_to_all(cot_rows, "depth", split_axis=1, concat_axis=0, tiled=True),
     )
     gd_all, ud_all, hid_all = (
-        lax.all_gather(gd_rows, "depth", axis=0, tiled=True),
+        ring_gather(gd_rows, "depth", 0),
         lax.all_gather(ud_rows, "depth", axis=0, tiled=True),
         lax.all_gather(hid_rows, "depth", axis=0, tiled=True),
     )

time: 808 us -> 767 us (0.949)
  waiting for transfers between devices: 632 us -> 577 us
    ppermute x0 -> x3, waiting for transfers between devices: none -> 98.4 us  [the longest x2 75.1 us: ring_gather(): lower.append(lax.ppermute(lower[-1] if lower else x, axis, pairs))]
    all_gather x1 -> x0, waiting for transfers between devices: 61.3 us -> none  [on_device(): lax.all_gather(gd_rows, 'depth', axis=0, tiled=True)]
    all_gather x1, waiting for transfers between devices: 49.2 us -> 10.3 us  [on_device(): lax.all_gather(ud_rows, 'depth', axis=0, tiled=True)]
    reduce_scatter x1, waiting for transfers between devices: 35.6 us -> 0.01 us  [on_device(): lax.psum_scatter(jnp.dot(hid_rows, down_full, preferred_element_type=jnp....]
    reduce_scatter x1, waiting for transfers between devices: 21.8 us -> 0.01 us  [on_device(): lax.psum_scatter(dot_nt(gd_rows, gate_full) + dot_nt(ud_rows, up_full), '...]
    reduce_scatter x1, waiting for transfers between devices: 1.3 us -> 14.4 us  [on_device(): lax.psum_scatter(jnp.dot(tok_rows, gate_full, preferred_element_type=jnp....]
    all_gather x1, waiting for transfers between devices: 122 us -> 110 us  [on_device(): lax.all_gather(gate_weight, 'depth', axis=0, tiled=True)]
    reduce_scatter x1, waiting for transfers between devices: 14.3 us -> 3.23 us  [on_device(): lax.psum_scatter(dot_nt(cot_rows, down_full), 'row', scatter_dimension=0,...]
  transfers between devices with their start and end apart: 16 -> 18, of which waited for: 14 -> 15; matrix products, arithmetic and copies ran while one was open for 12% -> 14% of each run, Pallas kernels for 0% -> 0%
where the time goes in v1:
time: 767 us; the launch traced here: 766 us
  waiting for transfers between devices  577 us (75%)
  matrix products  84.2 us (11%)
  blocking collectives  40.9 us (5%)
  local copies, waits for them, and re-layouts  24.9 us (3%)
  between operations  14 us (2%)
  other arithmetic  13.1 us (2%)
  starting transfers between devices  11.8 us (2%)
    all_gather x1, waiting for transfers between devices, on_device(): lax.all_gather(up_weight, 'depth', axis=0, tiled=True)  132 us
    all_gather x1, waiting for transfers between devices, on_device(): down_full = lax.all_gather(down_weight, 'depth', axis=1, tiled=True)  122 us
    all_gather x1, waiting for transfers between devices, on_device(): lax.all_gather(gate_weight, 'depth', axis=0, tiled=True)  110 us
    ppermute x2, waiting for transfers between devices, ring_gather(): lower.append(lax.ppermute(lower[-1] if lower else x, axis, pairs))  75.1 us
    all_gather x1, waiting for transfers between devices, on_device(): lax.all_gather(hid_rows, 'depth', axis=0, tiled=True)  49.2 us
    dot_general x3, matrix products, dot_nt(): lax.dot_general(left, right, (((1,), (1,)), ((), ())), preferred_element_...  31.9 us
    ppermute x1, waiting for transfers between devices, ring_gather(): upper.append(lax.ppermute(upper[-1] if upper else x, axis, back))  23.4 us
    dot_general x3, matrix products, dot_tn(): lax.dot_general(left, right, (((0,), (0,)), ((), ())), preferred_element_...  23.1 us
  transfers between devices with their start and end apart: 18, of which 15 were waited for; matrix products, arithmetic and copies ran while one was open for 14% of the time, Pallas kernels for 0%

profile of v1, /device:TPU:0, one launch (start us, length us, event | category | flops | bytes accessed | tf_op | source)
XLA Modules:
  0.0 765.7 jit_solution(16398707997000504063)
XLA Ops:
  7.2 0.0 all-gather.15.cloned.1.call-start
  7.2 0.7 all-gather.15.cloned.1.call-update
  7.9 0.0 all-gather.9.cloned.1.call-start
  8.0 0.7 all-gather.9.cloned.1.call-update
  8.7 0.0 all-gather.11.cloned.1.call-start
  8.7 0.7 all-gather.11.cloned.1.call-update
  9.4 0.0 reduce-scatter.12.cloned.1.call-start
  9.5 21.3 %all_gather.35 = bf16[192,2048]{1,0:T(8,128)(2,1)S(1)} all-gather(bf16[48,2048]{1,0:T(8,128)(2,1)S(1)} %copy-done.1), channel_id=1, replica_groups=mesh['row'=2,'col'=4,'depth'=4] {'col'}, dimensions={0}, use_global_device_ids=true | all-gather | bytes 983040 | tf_op jit(solution)/shard_map/all_gather | solution.py:60
  30.7 121.6 %all-gather.15.cloned.1.call-done = bf16[3584,2048]{1,0:T(8,128)(2,1)} async-done(((bf16[3584,512]{1,0:T(8,128)(2,1)}), bf16[3584,2048]{1,0:T(8,128)(2,1)}) %all-gather.15.cloned.1.call-update) | async-done | bytes 14680080 | tf_op jit(solution)/shard_map/all_gather | solution.py:57
  152.4 11.7 %fusion.6 = f32[192,3584]{1,0:T(8,128)} fusion(bf16[192,2048]{1,0:T(8,128)(2,1)S(1)} %all_gather.35, bf16[3584,2048]{1,0:T(8,128)(2,1)} %all-gather.15.cloned.1.call-done), kind=kOutput, calls=%fused_computation.22 | convolution fusion | flops 2818572288 | bytes 18219008 | tf_op jit(solution)/shard_map/dot_general | solution.py:36
  164.2 0.0 reduce-scatter.6.cloned.1.call-start
  164.2 19.6 %all_gather.30 = bf16[192,2048]{1,0:T(8,128)(2,1)S(1)} all-gather(bf16[48,2048]{1,0:T(8,128)(2,1)S(1)} %copy-done.2), channel_id=1, replica_groups=mesh['row'=2,'col'=4,'depth'=4] {'col'}, dimensions={0}, use_global_device_ids=true | all-gather | bytes 983040 | tf_op jit(solution)/shard_map/all_gather | solution.py:59
  183.8 110.4 %all-gather.9.cloned.1.call-done = bf16[2048,3584]{1,0:T(8,128)(2,1)} async-done(((bf16[512,3584]{1,0:T(8,128)(2,1)}), bf16[2048,3584]{1,0:T(8,128)(2,1)}) %all-gather.9.cloned.1.call-update) | async-done | bytes 14680080 | tf_op jit(solution)/shard_map/all_gather | solution.py:54
  294.2 9.8 %fusion.3 = f32[192,3584]{1,0:T(8,128)} fusion(bf16[192,2048]{1,0:T(8,128)(2,1)S(1)} %all_gather.30, bf16[2048,3584]{1,0:T(8,128)(2,1)} %all-gather.9.cloned.1.call-done), kind=kOutput, calls=%fused_computation.19 | convolution fusion | flops 2818572288 | bytes 18219008 | tf_op jit(solution)/shard_map/dot_general | solution.py:63
  304.0 0.0 reduce-scatter.6.cloned.1.call-update
  304.1 0.0 reduce-scatter.8.cloned.1.call-start
  304.1 132.0 %all-gather.11.cloned.1.call-done = bf16[2048,3584]{1,0:T(8,128)(2,1)} async-done(((bf16[512,3584]{1,0:T(8,128)(2,1)}), bf16[2048,3584]{1,0:T(8,128)(2,1)}) %all-gather.11.cloned.1.call-update) | async-done | bytes 14680080 | tf_op jit(solution)/shard_map/all_gather | solution.py:55
  436.1 9.7 %fusion.4 = f32[192,3584]{1,0:T(8,128)} fusion(bf16[192,2048]{1,0:T(8,128)(2,1)S(1)} %all_gather.30, bf16[2048,3584]{1,0:T(8,128)(2,1)} %all-gather.11.cloned.1.call-done), kind=kOutput, calls=%fused_computation.20 | convolution fusion | flops 2818572288 | bytes 18219008 | tf_op jit(solution)/shard_map/dot_general | solution.py:69
  445.8 0.0 reduce-scatter.8.cloned.1.call-update
  445.8 0.0 all-gather.13.cloned.1.call-start
  445.9 3.2 reduce-scatter.12.cloned.1.call-done
  449.1 14.4 %reduce-scatter.6.cloned.1.call-done = f32[96,3584]{1,0:T(8,128)} async-done(((f32[192,3584]{1,0:T(8,128)}), f32[96,3584]{1,0:T(8,128)}) %reduce-scatter.6.cloned.1.call-update) | async-done | bytes 1376272 | tf_op jit(solution)/shard_map/reduce_scatter | solution.py:62
  463.5 14.3 %reduce-scatter.8.cloned.1.call-done = f32[96,3584]{1,0:T(8,128)} async-done(((f32[192,3584]{1,0:T(8,128)}), f32[96,3584]{1,0:T(8,128)}) %reduce-scatter.8.cloned.1.call-update) | async-done | bytes 1376272 | tf_op jit(solution)/shard_map/reduce_scatter | solution.py:68
  477.8 4.2 multiply_convert_fusion
  482.0 0.0 all-gather.17.cloned.1.call-start
  482.1 0.7 all-gather.17.cloned.1.call-update
  482.8 0.0 all-gather.19.cloned.1.call-start
  482.8 0.7 all-gather.19.cloned.1.call-update
  483.5 0.2 reduce-scatter.10.cloned.1.call-start
  483.7 9.2 %all-gather.13.cloned.1.call-done = bf16[192,3584]{1,0:T(8,128)(2,1)} async-done(((bf16[96,3584]{1,0:T(8,128)(2,1)}), bf16[192,3584]{1,0:T(8,128)(2,1)}) %all-gather.13.cloned.1.call-update) | async-done | bytes 1376272 | tf_op jit(solution)/shard_map/all_gather | solution.py:74
  492.9 9.7 %fusion.5 = f32[192,2048]{1,0:T(8,128)} fusion(bf16[192,3584]{1,0:T(8,128)(2,1)} %all-gather.13.cloned.1.call-done, bf16[3584,2048]{1,0:T(8,128)(2,1)} %all-gather.15.cloned.1.call-done), kind=kOutput, calls=%fused_computation.21 | convolution fusion | flops 2818572288 | bytes 17629184 | tf_op jit(solution)/shard_map/dot_general | solution.py:84
  502.7 0.0 reduce-scatter.10.cloned.1.call-update
  502.7 0.0 reduce-scatter.14.cloned.1.call-start
  502.8 3.1 all-gather.17.cloned.1.call-done
  505.9 8.5 %fusion.7 = f32[192,2048]{1,0:T(8,128)S(1)} fusion(bf16[192,3584]{1,0:T(8,128)(2,1)} %all-gather.17.cloned.1.call-done, bf16[2048,3584]{1,0:T(8,128)(2,1)} %all-gather.9.cloned.1.call-done), kind=kOutput, calls=%fused_computation.23 | convolution fusion | flops 2818572288 | bytes 17629184 | tf_op jit(solution)/shard_map/dot_general | solution.py:36
  514.4 4.5 all-gather.19.cloned.1.call-done
  518.8 11.6 %convolution_add_fusion = f32[192,2048]{1,0:T(8,128)} fusion(f32[192,2048]{1,0:T(8,128)S(1)} %fusion.7, bf16[192,3584]{1,0:T(8,128)(2,1)} %all-gather.19.cloned.1.call-done, bf16[2048,3584]{1,0:T(8,128)(2,1)} %all-gather.11.cloned.1.call-done), kind=kOutput, calls=%fused_computation.4 | convolution fusion | flops 2818965504 | bytes 19202048 | tf_op jit(solution)/shard_map/dot_general | solution.py:36
  530.5 0.0 reduce-scatter.14.cloned.1.call-update
  530.5 0.0 all-gather.21.cloned.1.call-start
  530.5 0.5 all-gather.21.cloned.1.call-update
  531.1 0.0 all-gather.23.cloned.1.call-start
  531.1 0.7 all-gather.23.cloned.1.call-update
  531.8 1.8 collective-permute-start
  533.6 1.2 collective-permute-start.2
  534.8 31.1 %collective-permute-done = bf16[192,3584]{1,0:T(8,128)(2,1)} collective-permute-done((bf16[192,3584]{1,0:T(8,128)(2,1)S(1)}, bf16[192,3584]{1,0:T(8,128)(2,1)}, u32[]{:S(2)}, u32[]{:S(2)}) %collective-permute-start) | collective-permute-done | bytes 1376288 | tf_op jit(solution)/shard_map/ppermute | solution.py:20
  565.9 0.8 collective-permute-start.1
  566.7 1.0 copy.28
  567.7 3.6 all-to-all-start
  571.3 1.0 copy.27
  572.3 23.4 %collective-permute-done.2 = bf16[192,3584]{1,0:T(8,128)(2,1)} collective-permute-done((bf16[192,3584]{1,0:T(8,128)(2,1)S(1)}, bf16[192,3584]{1,0:T(8,128)(2,1)}, u32[]{:S(2)}, u32[]{:S(2)}) %collective-permute-start.2) | collective-permute-done | bytes 1376288 | tf_op jit(solution)/shard_map/ppermute | solution.py:22
  595.6 44.0 %collective-permute-done.1 = bf16[192,3584]{1,0:T(8,128)(2,1)} collective-permute-done((bf16[192,3584]{1,0:T(8,128)(2,1)}, bf16[192,3584]{1,0:T(8,128)(2,1)}, u32[]{:S(2)}, u32[]{:S(2)}) %collective-permute-start.1) | collective-permute-done | bytes 1376288 | tf_op jit(solution)/shard_map/ppermute | solution.py:20
  639.6 5.4 pad_maximum_fusion
  645.0 5.9 gather_fusion
  650.9 1.4 all-to-all-done
  652.3 3.7 all-to-all-start.1
  656.1 7.7 %convolution_bitcast_fusion.1 = f32[512,3584]{0,1:T(8,128)} fusion(bf16[4,192,3584]{2,1,0:T(8,128)(2,1)} %gather_fusion, bf16[192,4,512]{2,0,1:T(8,128)(2,1)S(1)} %all-to-all-done), kind=kOutput, calls=%fused_computation.2 | convolution fusion | flops 2818572288 | bytes 13631488 | tf_op jit(solution)/shard_map/dot_general | solution.py:30
  663.8 8.4 %copy.21 = f32[512,3584]{1,0:T(8,128)} copy(f32[512,3584]{0,1:T(8,128)} %convolution_bitcast_fusion.1) | data formatting | bytes 14680064
  672.1 1.7 convert_element_type.16
  673.8 1.7 convert_element_type.19
  675.5 10.3 %all-gather.21.cloned.1.call-done = bf16[768,3584]{1,0:T(8,128)(2,1)} async-done(((bf16[192,3584]{1,0:T(8,128)(2,1)}), bf16[768,3584]{1,0:T(8,128)(2,1)}) %all-gather.21.cloned.1.call-update) | async-done | bytes 5505040 | tf_op jit(solution)/shard_map/all_gather | solution.py:101
  685.8 7.7 %convolution_bitcast_fusion = f32[512,3584]{0,1:T(8,128)} fusion(bf16[768,3584]{1,0:T(8,128)(2,1)} %all-gather.21.cloned.1.call-done, bf16[768,512]{1,0:T(8,128)(2,1)S(1)} %bitcast.48), kind=kOutput, calls=%fused_computation.1 | convolution fusion | flops 2818572288 | bytes 13631488 | tf_op jit(solution)/shard_map/dot_general | solution.py:30
  693.5 8.8 %copy.22 = f32[512,3584]{1,0:T(8,128)} copy(f32[512,3584]{0,1:T(8,128)} %convolution_bitcast_fusion) | data formatting | bytes 14680064
  702.3 49.2 %all-gather.23.cloned.1.call-done = bf16[768,3584]{1,0:T(8,128)(2,1)} async-done(((bf16[192,3584]{1,0:T(8,128)(2,1)}), bf16[768,3584]{1,0:T(8,128)(2,1)}) %all-gather.23.cloned.1.call-update) | async-done | bytes 5505040 | tf_op jit(solution)/shard_map/all_gather | solution.py:102
  751.5 7.7 %fusion.8 = f32[3584,512]{1,0:T(8,128)} fusion(bf16[768,3584]{1,0:T(8,128)(2,1)} %all-gather.23.cloned.1.call-done, bf16[768,512]{1,0:T(8,128)(2,1)S(1)} %bitcast.49), kind=kOutput, calls=%fused_computation.24 | convolution fusion | flops 2818572288 | bytes 13631488 | tf_op jit(solution)/shard_map/dot_general | solution.py:30
  (13 shorter events, 0.1 us)
Async XLA Ops:
  7.2 145.2 %all-gather.15.cloned.1.call-start = ((), (), s32[]{:S(2)}) async-start(), calls=%async_computation.12 | async-start | bytes 18350080 | tf_op jit(solution)/shard_map/all_gather | solution.py:57
  7.9 1.5 copy-start.1
  7.9 286.3 %all-gather.9.cloned.1.call-start = ((), (), s32[]{:S(2)}) async-start(), calls=%async_computation.7 | async-start | bytes 18350080 | tf_op jit(solution)/shard_map/all_gather | solution.py:54
  8.7 427.4 %all-gather.11.cloned.1.call-start = ((), (), s32[]{:S(2)}) async-start(), calls=%async_computation.9 | async-start | bytes 18350080 | tf_op jit(solution)/shard_map/all_gather | solution.py:55
  9.4 439.7 %reduce-scatter.12.cloned.1.call-start = ((), (), s32[]{:S(2)}) async-start(), calls=%async_computation.14 | async-start | bytes 4128768 | tf_op jit(solution)/shard_map/reduce_scatter | solution.py:75
  30.7 133.5 %copy-start.2 = (bf16[48,2048]{1,0:T(8,128)(2,1)S(1)}, bf16[48,2048]{1,0:T(8,128)(2,1)}, u32[]{:S(2)}) copy-start(bf16[48,2048]{1,0:T(8,128)(2,1)} %param.5) | copy-start | bytes 589828
  164.2 299.3 %reduce-scatter.6.cloned.1.call-start = ((), (), s32[]{:S(2)}) async-start(), calls=%async_computation.8 | async-start | bytes 4128768 | tf_op jit(solution)/shard_map/reduce_scatter | solution.py:62
  304.1 173.7 %reduce-scatter.8.cloned.1.call-start = ((), (), s32[]{:S(2)}) async-start(), calls=%async_computation.10 | async-start | bytes 4128768 | tf_op jit(solution)/shard_map/reduce_scatter | solution.py:68
  445.8 47.1 %all-gather.13.cloned.1.call-start = ((), (), s32[]{:S(2)}) async-start(), calls=%async_computation.11 | async-start | bytes 2064384 | tf_op jit(solution)/shard_map/all_gather | solution.py:74
  482.0 23.8 %all-gather.17.cloned.1.call-start = ((), (), s32[]{:S(2)}) async-start(), calls=%async_computation.15 | async-start | bytes 2064384 | tf_op jit(solution)/shard_map/all_gather | solution.py:80
  482.8 36.0 %all-gather.19.cloned.1.call-start = ((), (), s32[]{:S(2)}) async-start(), calls=%async_computation.16 | async-start | bytes 2064384 | tf_op jit(solution)/shard_map/all_gather | solution.py:81
  483.5 188.6 %reduce-scatter.10.cloned.1.call-start = ((), (), s32[]{:S(2)}) async-start(), calls=%async_computation.13 | async-start | bytes 1966080 | tf_op jit(solution)/shard_map/reduce_scatter | solution.py:83
  502.7 171.1 %reduce-scatter.14.cloned.1.call-start = ((), (), s32[]{:S(2)}) async-start(), calls=%async_computation.17 | async-start | bytes 1966080 | tf_op jit(solution)/shard_map/reduce_scatter | solution.py:89
  530.5 1.4 copy-start
  530.5 155.3 %all-gather.21.cloned.1.call-start = ((), (), s32[]{:S(2)}) async-start(), calls=%async_computation.18 | async-start | bytes 6881280 | tf_op jit(solution)/shard_map/all_gather | solution.py:101
  531.1 220.4 %all-gather.23.cloned.1.call-start = ((), (), s32[]{:S(2)}) async-start(), calls=%async_computation.19 | async-start | bytes 6881280 | tf_op jit(solution)/shard_map/all_gather | solution.py:102
  531.8 34.1 %collective-permute-start = (bf16[192,3584]{1,0:T(8,128)(2,1)S(1)}, bf16[192,3584]{1,0:T(8,128)(2,1)}, u32[]{:S(2)}, u32[]{:S(2)}) collective-permute-start(bf16[192,3584]{1,0:T(8,128)(2,1)S(1)} %copy-done), channel_id=1, source_target_pairs={{0,1},{1,2},{2,3},{3,0},{4,5},{5,6},{6,7},{7,4},{8,9},{9,10},{10,1... | collective-permute-start | bytes 4128776 | tf_op jit(solution)/shard_map/ppermute | solution.py:20
  533.6 62.0 %collective-permute-start.2 = (bf16[192,3584]{1,0:T(8,128)(2,1)S(1)}, bf16[192,3584]{1,0:T(8,128)(2,1)}, u32[]{:S(2)}, u32[]{:S(2)}) collective-permute-start(bf16[192,3584]{1,0:T(8,128)(2,1)S(1)} %copy-done), channel_id=1, source_target_pairs={{1,0},{2,1},{3,2},{0,3},{5,4},{6,5},{7,6},{4,7},{9,8},{10,9},{11,1... | collective-permute-start | bytes 4128776 | tf_op jit(solution)/shard_map/ppermute | solution.py:22
  565.9 73.7 %collective-permute-start.1 = (bf16[192,3584]{1,0:T(8,128)(2,1)}, bf16[192,3584]{1,0:T(8,128)(2,1)}, u32[]{:S(2)}, u32[]{:S(2)}) collective-permute-start(bf16[192,3584]{1,0:T(8,128)(2,1)} %collective-permute-done), channel_id=1, source_target_pairs={{0,1},{1,2},{2,3},{3,0},{4,5},{5,6},{6,7},{7,4},{8,9},{9,10},{10,1... | collective-permute-start | bytes 4128776 | tf_op jit(solution)/shard_map/ppermute | solution.py:20
  567.7 84.7 %all-to-all-start = ((bf16[192,4,512]{2,0,1:T(8,128)(2,1)}), bf16[192,4,512]{2,0,1:T(8,128)(2,1)S(1)}, u32[]{:S(2)}, u32[]{:S(2)}) async-start(bf16[192,4,512]{2,0,1:T(8,128)(2,1)} %bitcast.44), calls=%async_computation.5 | async-start | bytes 1572864 | tf_op jit(solution)/shard_map/all_to_all | solution.py:96
  652.3 49.9 %all-to-all-start.1 = ((bf16[192,4,512]{2,0,1:T(8,128)(2,1)}), bf16[192,4,512]{2,0,1:T(8,128)(2,1)S(1)}, u32[]{:S(2)}, u32[]{:S(2)}) async-start(bf16[192,4,512]{2,0,1:T(8,128)(2,1)} %bitcast.43), calls=%async_computation.6 | async-start | bytes 1572864 | tf_op jit(solution)/shard_map/all_to_all | solution.py:97
Sparse Core Ops, SparseCore 0:
  9.8 142.5 all-gather.14
  154.2 139.9 all-gather.8
  296.1 139.9 all-gather.10
  438.8 10.3 reduce-scatter.11
  451.9 11.5 reduce-scatter.5
  466.1 11.5 reduce-scatter.7
  482.1 10.7 all-gather.12
  495.1 10.6 all-gather.16
  508.0 10.7 all-gather.18
  521.1 36.4 reduce-scatter.9
  560.0 34.2 reduce-scatter.13
  596.1 89.6 all-gather.20
  687.8 63.6 all-gather.22
